TPU v7x, 256 devices: a whole 4x4x8 slice. The times are simulated.
256 devices in a mesh: req: 8 (over z_lo, core), tile: 16 (over x, y), blk: 2 (over z_hi).
Axes of the slice: x: 4, y: 4, z: 8 (z_hi: 2, z_lo: 4; z = z_hi * 4 + z_lo), core: 2. Of those that a mesh axis runs over, the one named last changes fastest.
Arguments:
- image_tokens: bfloat16 [16, 1024, 1536], P(('req', 'blk'), 'tile'), may hold values from -6 to 6
- latent: float32 [16, 512, 128], P(('req', 'blk'), 'tile'), may hold values from -6 to 6
- modulation: float32 [16, 8, 1536], P(('req', 'blk')), may hold values from -3 to 3
- text_kv: bfloat16 [16, 154, 2, 1536], P(('req', 'blk')), as said below
- text_len: int32 [16], P(('req', 'blk')), may hold values from 38 to 154, as said below
- timestep: int32 [16], P(('req', 'blk')), may hold values from 0 to 7
- w_qkv: bfloat16 [1536, 3, 1536], P(None, None, 'tile'), may hold values from -0.15625 to 0.15625
- w_out: bfloat16 [1536, 1536], P('tile'), may hold values from -0.15625 to 0.15625
- w_up: bfloat16 [1536, 6144], P(None, 'tile'), may hold values from -0.15625 to 0.15625
- w_down: bfloat16 [6144, 1536], P('tile'), may hold values from -0.078125 to 0.078125
- w_final: bfloat16 [1536, 64], replicated, may hold values from -0.15625 to 0.15625
Outputs:
- image_state: bfloat16 [16, 1024, 1536], P(('req', 'blk'), 'tile')
- latent_next: float32 [16, 512, 128], P(('req', 'blk'), 'tile')
Inputs may be any that keep to these rules, and one draw needn't show every extreme that they name: `text_len`: each request has 38 to 154 live text tokens; some request has 154 and some 154 // 4. `text_kv`: keys and values of text tokens, finite.
All inputs are finite; a program needn't handle non-finite values.
Results may differ from a plain program's by a relative error of at most 0.014.
Values may be sent and summed in bfloat16 or wider, within the bound.
No kernel may reach another device: no remote copies, remote signals or barrier semaphores. Data moves between devices by JAX's collectives and lax.ppermute only.
A program may use at most 64 MiB of HBM per device.

v0:
```python
import jax
import jax.numpy as jnp
from jax import lax
from jax.sharding import PartitionSpec as P

HEAD_DIM = 64
TXT = 154
STEPS = 8


def normed(value, shift, scale):
    full = value.astype(jnp.float32)
    mean = jnp.mean(full, axis=-1, keepdims=True)
    spread = jnp.mean(jnp.square(full - mean), axis=-1, keepdims=True)
    return (full - mean) * lax.rsqrt(spread + 1e-06) * (1.0 + scale) + shift


def sigma_at(index):
    frac = 1.0 - index.astype(jnp.float32) / STEPS
    return 3.0 * frac / (1.0 + 2.0 * frac)


def on_device(
    image_tokens,
    latent,
    modulation,
    text_kv,
    text_len,
    timestep,
    w_qkv,
    w_out,
    w_up,
    w_down,
    w_final,
):
    tokens = image_tokens[0]
    mods = modulation[0]
    rows_here = tokens.shape[0]
    width = tokens.shape[1]
    heads = width // HEAD_DIM
    scale_factor = HEAD_DIM ** (-0.5)
    h1 = normed(tokens, mods[0], mods[1]).astype(jnp.bfloat16)
    qkv_all = jnp.einsum(
        "nd,dkc->nkc",
        lax.all_gather(h1, "tile", axis=0, tiled=True),
        w_qkv,
        preferred_element_type=jnp.float32,
    ).astype(jnp.bfloat16)
    qkv = lax.all_to_all(qkv_all, "tile", split_axis=0, concat_axis=2, tiled=True)
    query = qkv[:, 0].reshape(rows_here, heads, HEAD_DIM)
    keyval = qkv[:, 1:]
    text_pair = text_kv[0]
    text_keys = text_pair[:, 0].reshape(TXT, heads, HEAD_DIM)
    text_values = text_pair[:, 1].reshape(TXT, heads, HEAD_DIM)
    live = jnp.arange(TXT, dtype=jnp.int32) < text_len[0]
    text_scores = (
        jnp.einsum("qhe,khe->hqk", query, text_keys, preferred_element_type=jnp.float32)
        * scale_factor
    )
    text_scores = jnp.where(live[None, None, :], text_scores, -jnp.inf)
    top_start = jnp.max(text_scores, axis=-1)
    text_weights = jnp.exp(text_scores - top_start[:, :, None])
    total_start = jnp.sum(text_weights, axis=-1)
    acc_start = jnp.einsum(
        "hqk,khe->hqe",
        text_weights.astype(jnp.bfloat16),
        text_values,
        preferred_element_type=jnp.float32,
    )
    piece = lax.all_gather(keyval, "tile", axis=0, tiled=True)
    total = total_start
    acc = acc_start
    count = piece.shape[0]
    piece_keys = piece[:, 0].reshape(count, heads, HEAD_DIM)
    piece_values = piece[:, 1].reshape(count, heads, HEAD_DIM)
    scores = (
        jnp.einsum("qhe,khe->hqk", query, piece_keys, preferred_element_type=jnp.float32)
        * scale_factor
    )
    new_top = jnp.maximum(top_start, jnp.max(scores, axis=-1))
    factor = jnp.exp(top_start - new_top)
    weights = jnp.exp(scores - new_top[:, :, None])
    total = total * factor + jnp.sum(weights, axis=-1)
    acc = acc * factor[:, :, None] + jnp.einsum(
        "hqk,khe->hqe",
        weights.astype(jnp.bfloat16),
        piece_values,
        preferred_element_type=jnp.float32,
    )
    summed = acc / total[:, :, None]
    attended = jnp.transpose(summed, (1, 0, 2)).reshape(rows_here, width).astype(jnp.bfloat16)
    columns = lax.all_to_all(attended, "tile", split_axis=1, concat_axis=0, tiled=True)
    block_rows = columns
    proj = lax.psum_scatter(
        jnp.dot(block_rows, w_out, preferred_element_type=jnp.float32).astype(jnp.bfloat16),
        "tile",
        scatter_dimension=0,
        tiled=True,
    ).astype(jnp.float32)
    second = (tokens.astype(jnp.float32) + mods[2] * proj).astype(jnp.bfloat16)
    h2 = normed(second, mods[3], mods[4]).astype(jnp.bfloat16)
    hidden = jax.nn.gelu(
        jnp.dot(
            lax.all_gather(h2, "tile", axis=0, tiled=True), w_up, preferred_element_type=jnp.float32
        ),
        approximate=True,
    ).astype(jnp.bfloat16)
    block_rows = hidden
    ffn = lax.psum_scatter(
        jnp.dot(block_rows, w_down, preferred_element_type=jnp.float32).astype(jnp.bfloat16),
        "tile",
        scatter_dimension=0,
        tiled=True,
    ).astype(jnp.float32)
    state = (second.astype(jnp.float32) + mods[5] * ffn).astype(jnp.bfloat16)
    final_in = normed(state, mods[6], mods[7]).astype(jnp.bfloat16)
    velocity = jnp.dot(final_in, w_final, preferred_element_type=jnp.float32)
    step_index = timestep[0]
    delta = sigma_at(step_index + 1) - sigma_at(step_index)
    moved = latent[0] + delta * velocity.reshape(rows_here // 2, 2 * velocity.shape[1])
    return (state[None], moved[None])


def solution(mesh):
    in_specs = (
        P(("req", "blk"), "tile", None),
        P(("req", "blk"), "tile", None),
        P(("req", "blk"), None, None),
        P(("req", "blk"), None, None, None),
        P(("req", "blk")),
        P(("req", "blk")),
        P(None, None, "tile"),
        P("tile", None),
        P(None, "tile"),
        P("tile", None),
        P(),
    )
    out_specs = (P(("req", "blk"), "tile", None), P(("req", "blk"), "tile", None))
    return jax.shard_map(
        on_device, mesh=mesh, in_specs=in_specs, out_specs=out_specs, check_vma=False
    )
```

profile of v0, /device:TPU:32, one launch (start us, length us, event | category | flops | bytes accessed | tf_op | source)
XLA Modules:
  0.0 429.9 jit_solution(14177773688961563732)
XLA Ops:
  7.2 1.4 add_reduce_fusion
  9.7 1.2 fusion.46
  10.8 1.8 fusion.49
  12.7 55.7 %all-gather.4.cloned.1.call-done = bf16[1024,1536]{1,0:T(8,128)(2,1)} async-done(((bf16[64,1536]{1,0:T(8,128)(2,1)}), bf16[1024,1536]{1,0:T(8,128)(2,1)}) %all-gather.4.cloned.1.call-update) | async-done | bytes 3145744 | tf_op jit(solution)/shard_map/all_gather | solution.py:45
  68.3 3.2 fusion.74
  72.4 20.9 %all_to_all.34 = bf16[1024,3,96]{2,1,0:T(4,128)(2,1)S(1)} all-to-all(bf16[1024,3,96]{2,1,0:T(4,128)(2,1)S(1)} %copy.25), channel_id=1, replica_groups=mesh['req'=8,'tile'=16,'blk'=2] {'tile'}, dimensions={0} | all-to-all | bytes 1179648 | tf_op jit(solution)/shard_map/all_to_all | solution.py:49
  95.9 2.1 fusion.70
  98.0 3.1 copy.28
  101.8 1.9 copy.30
  103.9 1.6 fusion.71
  106.0 54.2 %all-gather.6.cloned.1.call-done = bf16[1024,2,1536]{2,0,1:T(8,128)(2,1)} async-done(((bf16[64,2,1536]{2,0,1:T(8,128)(2,1)}), bf16[1024,2,1536]{2,0,1:T(8,128)(2,1)}) %all-gather.6.cloned.1.call-update) | async-done | bytes 6291472 | tf_op jit(solution)/shard_map/all_gather | solution.py:70
  160.2 5.9 %fusion.69 = (bf16[1024,1,1536]{2,0,1:T(8,128)(2,1)}, bf16[1024,1,1536]{2,0,1:T(8,128)(2,1)}) fusion(bf16[1024,2,1536]{2,0,1:T(8,128)(2,1)} %all-gather.6.cloned.1.call-done), kind=kLoop, calls=%fused_computation.94 | loop fusion | bytes 12582912 | tf_op jit(solution)/shard_map/slice | solution.py:74
  166.1 4.6 %copy.33 = bf16[1024,1,1536]{0,2,1:T(8,128)(2,1)} copy(bf16[1024,1,1536]{2,0,1:T(8,128)(2,1)} %get-tuple-element.17) | data formatting | bytes 6291456 | tf_op jit(solution)/shard_map/slice | solution.py:75
  170.8 4.7 %copy.31 = bf16[1024,1,1536]{0,2,1:T(8,128)(2,1)} copy(bf16[1024,1,1536]{2,0,1:T(8,128)(2,1)} %get-tuple-element.16) | data formatting | bytes 6291456 | tf_op jit(solution)/shard_map/slice | solution.py:74
  175.5 2.9 multiply_reduce_fusion
  178.4 1.3 fusion
  180.3 1.6 fusion.16
  183.4 13.6 %all_to_all.35 = bf16[64,16,96]{2,0,1:T(8,128)(2,1)S(1)} all-to-all(bf16[64,16,96]{2,0,1:T(8,128)(2,1)S(1)} %copy.35), channel_id=1, replica_groups=mesh['req'=8,'tile'=16,'blk'=2] {'tile'}, dimensions={1} | all-to-all | bytes 393216 | tf_op jit(solution)/shard_map/all_to_all | solution.py:92
  196.9 2.6 convolution_convert_fusion.1
  199.7 79.1 %reduce-scatter.3.cloned.1.call-done = bf16[64,1536]{1,0:T(8,128)(2,1)} async-done(((bf16[1024,1536]{1,0:T(8,128)(2,1)}), bf16[64,1536]{1,0:T(8,128)(2,1)}) %reduce-scatter.3.cloned.1.call-update) | async-done | bytes 196624 | tf_op jit(solution)/shard_map/reduce_scatter | solution.py:94
  278.7 1.1 convert_reduce_fusion
  281.0 52.9 %all-gather.8.cloned.1.call-done = bf16[1024,1536]{1,0:T(8,128)(2,1)} async-done(((bf16[64,1536]{1,0:T(8,128)(2,1)}), bf16[1024,1536]{1,0:T(8,128)(2,1)}) %all-gather.8.cloned.1.call-update) | async-done | bytes 3145744 | tf_op jit(solution)/shard_map/all_gather | solution.py:104
  333.9 7.2 %convolution_convert_fusion = bf16[1024,1536]{1,0:T(8,128)(2,1)} fusion(bf16[384,1536]{1,0:T(8,128)(2,1)S(1)} %copy-done, bf16[1024,1536]{1,0:T(8,128)(2,1)} %all-gather.8.cloned.1.call-done, bf16[1536,384]{1,0:T(8,128)(2,1)S(1)} %copy-done.9), kind=kOutput, calls=%fused_computation.4 | convolution fusion | flops 2421030912 | bytes 8650752 | tf_op jit(solution)/shard_map/dot_general | solution.py:110
  341.9 79.1 %reduce-scatter.5.cloned.1.call-done = bf16[64,1536]{1,0:T(8,128)(2,1)} async-done(((bf16[1024,1536]{1,0:T(8,128)(2,1)}), bf16[64,1536]{1,0:T(8,128)(2,1)}) %reduce-scatter.5.cloned.1.call-update) | async-done | bytes 196624 | tf_op jit(solution)/shard_map/reduce_scatter | solution.py:109
  (63 shorter events, 10.8 us)
Async XLA Ops:
  7.2 326.8 %copy-start = (bf16[384,1536]{1,0:T(8,128)(2,1)S(1)}, bf16[384,1536]{1,0:T(8,128)(2,1)}, u32[]{:S(2)}) copy-start(bf16[384,1536]{1,0:T(8,128)(2,1)} %param.20) | copy-start | bytes 3538948
  7.2 61.2 %all-gather.4.cloned.1.call-start = ((), (), s32[]{:S(2)}) async-start(), calls=%async_computation.4 | async-start | bytes 3342336 | tf_op jit(solution)/shard_map/all_gather | solution.py:45
  12.6 147.6 %all-gather.6.cloned.1.call-start = ((), (), s32[]{:S(2)}) async-start(), calls=%async_computation.5 | async-start | bytes 6684672 | tf_op jit(solution)/shard_map/all_gather | solution.py:70
  93.3 2.6 copy-start.2
  94.9 1.1 copy-start.4
  95.8 183.0 %reduce-scatter.3.cloned.1.call-start = ((), (), s32[]{:S(2)}) async-start(), calls=%async_computation.6 | async-start | bytes 3342336 | tf_op jit(solution)/shard_map/reduce_scatter | solution.py:94
  95.9 7.8 %slice-start = ((bf16[64,3,1536]{2,0,1:T(8,128)(2,1)}), bf16[64,1,1536]{2,0,1:T(8,128)(2,1)S(1)}, s32[]{:S(2)}) async-start(bf16[64,3,1536]{2,0,1:T(8,128)(2,1)} %copy-done.4), calls=%async_computation.9 | async-start | bytes 393216 | tf_op jit(solution)/shard_map/slice | solution.py:50
  178.4 1.9 copy-start.1
  180.3 1.6 copy-start.5
  181.9 15.0 %copy-start.7 = (bf16[96,1536]{1,0:T(8,128)(2,1)S(1)}, bf16[96,1536]{1,0:T(8,128)(2,1)}, u32[]{:S(2)}) copy-start(bf16[96,1536]{1,0:T(8,128)(2,1)} %param.18) | copy-start | bytes 884740
  196.9 81.8 %copy-start.3 = (bf16[1,64,1536]{2,1,0:T(8,128)(2,1)S(1)}, bf16[1,64,1536]{2,1,0:T(8,128)(2,1)}, u32[]{:S(2)}) copy-start(bf16[1,64,1536]{2,1,0:T(8,128)(2,1)} %param.11) | copy-start | bytes 589828
  199.6 134.3 %copy-start.9 = (bf16[1536,384]{1,0:T(8,128)(2,1)S(1)}, bf16[1536,384]{1,0:T(8,128)(2,1)}, u32[]{:S(2)}) copy-start(bf16[1536,384]{1,0:T(8,128)(2,1)} %param.19) | copy-start | bytes 3538948
  199.6 134.3 %all-gather.8.cloned.1.call-start = ((), (), s32[]{:S(2)}) async-start(), calls=%async_computation.7 | async-start | bytes 3342336 | tf_op jit(solution)/shard_map/all_gather | solution.py:104
  280.9 140.1 %reduce-scatter.5.cloned.1.call-start = ((), (), s32[]{:S(2)}) async-start(), calls=%async_computation.8 | async-start | bytes 3342336 | tf_op jit(solution)/shard_map/reduce_scatter | solution.py:109
  341.1 81.3 %copy-start.10 = (bf16[1536,64]{0,1:T(8,128)(2,1)S(1)}, bf16[1536,64]{0,1:T(8,128)(2,1)}, u32[]{:S(2)}) copy-start(bf16[1536,64]{0,1:T(8,128)(2,1)} %param.21) | copy-start | bytes 589828
  341.1 81.7 %copy-start.8 = (f32[1,32,128]{2,1,0:T(8,128)S(1)}, f32[1,32,128]{2,1,0:T(8,128)}, u32[]{:S(2)}) copy-start(f32[1,32,128]{2,1,0:T(8,128)} %param.12) | copy-start | bytes 49156
  422.2 1.2 copy-start.6
Sparse Core Ops, SparseCore 0:
  12.7 55.5 all-gather.3
  95.9 64.2 all-gather.5
  199.7 78.9 reduce-scatter.2
  281.6 52.2 all-gather.7
  341.3 79.7 reduce-scatter.4
where the time goes:
time: 431 us; the launch traced here: 430 us
  waiting for transfers between devices  321 us (74%)
  blocking collectives  34.5 us (8%)
  local copies, waits for them, and re-layouts  27 us (6%)
  matrix products  20.2 us (5%)
  between operations  15.4 us (4%)
  other arithmetic  11.4 us (3%)
    reduce_scatter x1, waiting for transfers between devices, on_device(): lax.psum_scatter(jnp.dot(block_rows, w_down, preferred_element_type=jnp.f...  79.1 us
    reduce_scatter x1, waiting for transfers between devices, on_device(): lax.psum_scatter(jnp.dot(block_rows, w_out, preferred_element_type=jnp.fl...  79.1 us
    all_gather x1, waiting for transfers between devices, on_device(): lax.all_gather(h1, 'tile', axis=0, tiled=True)  55.7 us
    all_gather x1, waiting for transfers between devices, on_device(): piece = lax.all_gather(keyval, 'tile', axis=0, tiled=True)  54.2 us
    all_gather x1, waiting for transfers between devices, on_device(): lax.all_gather(h2, 'tile', axis=0, tiled=True)  52.9 us
    all_to_all x1, blocking collectives, on_device(): lax.all_to_all(qkv_all, 'tile', split_axis=0, concat_axis=2, tiled=True)  20.9 us
    all_to_all x1, blocking collectives, on_device(): lax.all_to_all(attended, 'tile', split_axis=1, concat_axis=0, tiled=True)  13.6 us
    slice x2, local copies, waits for them, and re-layouts, on_device(): piece_keys = piece[:, 0].reshape(count, heads, HEAD_DIM)  10.6 us
  transfers between devices with their start and end apart: 5, of which 5 were waited for; matrix products, arithmetic and copies ran while one was open for 2% of the time, Pallas kernels for 0%

commit v1 on v0

--- a/solution.py
+++ b/solution.py
@@ -6,6 +6,27 @@
 HEAD_DIM = 64
 TXT = 154
 STEPS = 8
+
+
+def ring_gather(value, axis, dim):
+    length, mine, width = (lax.axis_size(axis), lax.axis_index(axis), value.shape[dim])
+    forward = [(i, (i + 1) % length) for i in range(length)]
+    behind = [(i, (i - 1) % length) for i in range(length)]
+    filled = jnp.zeros((*value.shape[:dim], length * width, *value.shape[dim + 1 :]), value.dtype)
+    filled = lax.dynamic_update_slice_in_dim(filled, value, mine * width, axis=dim)
+    from_left = from_right = value
+    halfway = length // 2
+    for step in range(1, halfway + 1):
+        from_left = lax.ppermute(from_left, axis, forward)
+        filled = lax.dynamic_update_slice_in_dim(
+            filled, from_left, (mine - step) % length * width, axis=dim
+        )
+        if step < length - halfway:
+            from_right = lax.ppermute(from_right, axis, behind)
+            filled = lax.dynamic_update_slice_in_dim(
+                filled, from_right, (mine + step) % length * width, axis=dim
+            )
+    return filled
 
 
 def normed(value, shift, scale):
@@ -41,10 +62,7 @@
     scale_factor = HEAD_DIM ** (-0.5)
     h1 = normed(tokens, mods[0], mods[1]).astype(jnp.bfloat16)
     qkv_all = jnp.einsum(
-        "nd,dkc->nkc",
-        lax.all_gather(h1, "tile", axis=0, tiled=True),
-        w_qkv,
-        preferred_element_type=jnp.float32,
+        "nd,dkc->nkc", ring_gather(h1, "tile", 0), w_qkv, preferred_element_type=jnp.float32
     ).astype(jnp.bfloat16)
     qkv = lax.all_to_all(qkv_all, "tile", split_axis=0, concat_axis=2, tiled=True)
     query = qkv[:, 0].reshape(rows_here, heads, HEAD_DIM)

time: 431 us -> 451 us (1.046)
  starting transfers between devices: 0.21 us -> 38.1 us
  waiting for transfers between devices: 321 us -> 294 us
  local copies, waits for them, and re-layouts: 27 us -> 40.9 us
  blocking collectives: 34.5 us -> 29.1 us
    all_gather x1 -> x0, waiting for transfers between devices: 55.7 us -> none  [on_device(): lax.all_gather(h1, 'tile', axis=0, tiled=True)]
    ppermute x0 -> x15, starting transfers between devices: none -> 37.7 us  [the longest x7 36.1 us: ring_gather(): from_right = lax.ppermute(from_right, axis, behind)]
    ppermute x0 -> x15, waiting for transfers between devices: none -> 28 us  [the longest x8 28 us: ring_gather(): from_left = lax.ppermute(from_left, axis, forward)]
    dynamic_update_slice x0 -> x15, local copies, waits for them, and re-layouts: none -> 10.3 us  [the longest x8 5.48 us: ring_gather(): lax.dynamic_update_slice_in_dim(filled, from_left, (mine - step) % length...]
    all_to_all x1, blocking collectives: 20.9 us -> 15.5 us  [on_device(): lax.all_to_all(qkv_all, 'tile', split_axis=0, concat_axis=2, tiled=True)]
  transfers between devices with their start and end apart: 5 -> 19, of which waited for: 5 -> 12; matrix products, arithmetic and copies ran while one was open for 2% -> 4% of each run, Pallas kernels for 0% -> 0%
where the time goes in v1:
time: 451 us; the launch traced here: 450 us
  waiting for transfers between devices  294 us (65%)
  local copies, waits for them, and re-layouts  40.9 us (9%)
  starting transfers between devices  38.1 us (8%)
  blocking collectives  29.1 us (6%)
  matrix products  21.2 us (5%)
  between operations  15.5 us (3%)
  other arithmetic  11.6 us (3%)
    reduce_scatter x1, waiting for transfers between devices, on_device(): lax.psum_scatter(jnp.dot(block_rows, w_down, preferred_element_type=jnp.f...  79.1 us
    reduce_scatter x1, waiting for transfers between devices, on_device(): lax.psum_scatter(jnp.dot(block_rows, w_out, preferred_element_type=jnp.fl...  78.8 us
    all_gather x1, waiting for transfers between devices, on_device(): piece = lax.all_gather(keyval, 'tile', axis=0, tiled=True)  54.8 us
    all_gather x1, waiting for transfers between devices, on_device(): lax.all_gather(h2, 'tile', axis=0, tiled=True)  53.1 us
    ppermute x7, starting transfers between devices, ring_gather(): from_right = lax.ppermute(from_right, axis, behind)  36.1 us
    ppermute x8, waiting for transfers between devices, ring_gather(): from_left = lax.ppermute(from_left, axis, forward)  28 us
    all_to_all x1, blocking collectives, on_device(): lax.all_to_all(qkv_all, 'tile', split_axis=0, concat_axis=2, tiled=True)  15.5 us
    all_to_all x1, blocking collectives, on_device(): lax.all_to_all(attended, 'tile', split_axis=1, concat_axis=0, tiled=True)  13.6 us
  transfers between devices with their start and end apart: 19, of which 12 were waited for; matrix products, arithmetic and copies ran while one was open for 4% of the time, Pallas kernels for 0%

profile of v1, /device:TPU:32, one launch (start us, length us, event | category | flops | bytes accessed | tf_op | source)
XLA Modules:
  0.0 450.3 jit_solution(7710923987586129080)
XLA Ops:
  15.7 3.8 collective-permute-start.1
  19.5 4.8 %collective-permute-done = bf16[64,1536]{1,0:T(8,128)(2,1)S(1)} collective-permute-done((bf16[64,1536]{1,0:T(8,128)(2,1)S(1)}, bf16[64,1536]{1,0:T(8,128)(2,1)S(1)}, u32[]{:S(2)}, u32[]{:S(2)}) %collective-permute-start) | collective-permute-done | bytes 196640 | tf_op jit(solution)/shard_map/ppermute | solution.py:20
  24.3 5.3 %collective-permute-start.3 = (bf16[64,1536]{1,0:T(8,128)(2,1)S(1)}, bf16[64,1536]{1,0:T(8,128)(2,1)S(1)}, u32[]{:S(2)}, u32[]{:S(2)}) collective-permute-start(bf16[64,1536]{1,0:T(8,128)(2,1)S(1)} %collective-permute-done.1), channel_id=1, source_target_pairs={{0,30},{2,0},{4,2},{6,4},{8,6},{10,8},{12,10},{14,12},{16,14},{18,... | collective-permute-start | bytes 589832 | tf_op jit(solution)/shard_map/ppermute | solution.py:25
  33.6 5.3 %collective-permute-start.5 = (bf16[64,1536]{1,0:T(8,128)(2,1)S(1)}, bf16[64,1536]{1,0:T(8,128)(2,1)S(1)}, u32[]{:S(2)}, u32[]{:S(2)}) collective-permute-start(bf16[64,1536]{1,0:T(8,128)(2,1)S(1)} %collective-permute-done.3), channel_id=1, source_target_pairs={{0,30},{2,0},{4,2},{6,4},{8,6},{10,8},{12,10},{14,12},{16,14},{18,... | collective-permute-start | bytes 589832 | tf_op jit(solution)/shard_map/ppermute | solution.py:25
  42.5 5.3 %collective-permute-start.7 = (bf16[64,1536]{1,0:T(8,128)(2,1)S(1)}, bf16[64,1536]{1,0:T(8,128)(2,1)S(1)}, u32[]{:S(2)}, u32[]{:S(2)}) collective-permute-start(bf16[64,1536]{1,0:T(8,128)(2,1)S(1)} %collective-permute-done.5), channel_id=1, source_target_pairs={{0,30},{2,0},{4,2},{6,4},{8,6},{10,8},{12,10},{14,12},{16,14},{18,... | collective-permute-start | bytes 589832 | tf_op jit(solution)/shard_map/ppermute | solution.py:25
  51.5 5.3 %collective-permute-start.9 = (bf16[64,1536]{1,0:T(8,128)(2,1)S(1)}, bf16[64,1536]{1,0:T(8,128)(2,1)S(1)}, u32[]{:S(2)}, u32[]{:S(2)}) collective-permute-start(bf16[64,1536]{1,0:T(8,128)(2,1)S(1)} %collective-permute-done.7), channel_id=1, source_target_pairs={{0,30},{2,0},{4,2},{6,4},{8,6},{10,8},{12,10},{14,12},{16,14},{18,... | collective-permute-start | bytes 589832 | tf_op jit(solution)/shard_map/ppermute | solution.py:25
  60.5 5.3 %collective-permute-start.11 = (bf16[64,1536]{1,0:T(8,128)(2,1)S(1)}, bf16[64,1536]{1,0:T(8,128)(2,1)S(1)}, u32[]{:S(2)}, u32[]{:S(2)}) collective-permute-start(bf16[64,1536]{1,0:T(8,128)(2,1)S(1)} %collective-permute-done.9), channel_id=1, source_target_pairs={{0,30},{2,0},{4,2},{6,4},{8,6},{10,8},{12,10},{14,12},{16,14},{18,... | collective-permute-start | bytes 589832 | tf_op jit(solution)/shard_map/ppermute | solution.py:25
  69.9 5.6 %collective-permute-start.13 = (bf16[64,1536]{1,0:T(8,128)(2,1)S(1)}, bf16[64,1536]{1,0:T(8,128)(2,1)S(1)}, u32[]{:S(2)}, u32[]{:S(2)}) collective-permute-start(bf16[64,1536]{1,0:T(8,128)(2,1)S(1)} %collective-permute-done.11), channel_id=1, source_target_pairs={{0,30},{2,0},{4,2},{6,4},{8,6},{10,8},{12,10},{14,12},{16,14},{18,... | collective-permute-start | bytes 589832 | tf_op jit(solution)/shard_map/ppermute | solution.py:25
  76.9 3.6 collective-permute-done.12
  81.9 7.6 %collective-permute-done.14 = bf16[64,1536]{1,0:T(8,128)(2,1)S(1)} collective-permute-done((bf16[64,1536]{1,0:T(8,128)(2,1)S(1)}, bf16[64,1536]{1,0:T(8,128)(2,1)S(1)}, u32[]{:S(2)}, u32[]{:S(2)}) %collective-permute-start.14) | collective-permute-done | bytes 196640 | tf_op jit(solution)/shard_map/ppermute | solution.py:20
  90.2 3.2 fusion.75
  94.2 15.5 %all_to_all.34 = bf16[1024,3,96]{2,1,0:T(4,128)(2,1)S(1)} all-to-all(bf16[1024,3,96]{2,1,0:T(4,128)(2,1)S(1)} %copy.25), channel_id=1, replica_groups=mesh['req'=8,'tile'=16,'blk'=2] {'tile'}, dimensions={0} | all-to-all | bytes 1179648 | tf_op jit(solution)/shard_map/all_to_all | solution.py:67
  116.2 3.1 copy.28
  124.7 54.8 %all-gather.3.cloned.1.call-done = bf16[1024,2,1536]{2,0,1:T(8,128)(2,1)} async-done(((bf16[64,2,1536]{2,0,1:T(8,128)(2,1)}), bf16[1024,2,1536]{2,0,1:T(8,128)(2,1)}) %all-gather.3.cloned.1.call-update) | async-done | bytes 6291472 | tf_op jit(solution)/shard_map/all_gather | solution.py:88
  179.5 5.9 %fusion.70 = (bf16[1024,1,1536]{2,0,1:T(8,128)(2,1)}, bf16[1024,1,1536]{2,0,1:T(8,128)(2,1)}) fusion(bf16[1024,2,1536]{2,0,1:T(8,128)(2,1)} %all-gather.3.cloned.1.call-done), kind=kLoop, calls=%fused_computation.110 | loop fusion | bytes 12582912 | tf_op jit(solution)/shard_map/slice | solution.py:92
  185.4 4.6 %copy.33 = bf16[1024,1,1536]{0,2,1:T(8,128)(2,1)} copy(bf16[1024,1,1536]{2,0,1:T(8,128)(2,1)} %get-tuple-element.19) | data formatting | bytes 6291456 | tf_op jit(solution)/shard_map/slice | solution.py:93
  190.0 4.7 %copy.31 = bf16[1024,1,1536]{0,2,1:T(8,128)(2,1)} copy(bf16[1024,1,1536]{2,0,1:T(8,128)(2,1)} %get-tuple-element.18) | data formatting | bytes 6291456 | tf_op jit(solution)/shard_map/slice | solution.py:92
  194.7 2.9 multiply_reduce_fusion
  202.6 13.6 %all_to_all.35 = bf16[64,16,96]{2,0,1:T(8,128)(2,1)S(1)} all-to-all(bf16[64,16,96]{2,0,1:T(8,128)(2,1)S(1)} %copy.35), channel_id=1, replica_groups=mesh['req'=8,'tile'=16,'blk'=2] {'tile'}, dimensions={1} | all-to-all | bytes 393216 | tf_op jit(solution)/shard_map/all_to_all | solution.py:110
  216.2 3.6 convolution_convert_fusion.1
  220.1 78.8 %reduce-scatter.3.cloned.1.call-done = bf16[64,1536]{1,0:T(8,128)(2,1)} async-done(((bf16[1024,1536]{1,0:T(8,128)(2,1)}), bf16[64,1536]{1,0:T(8,128)(2,1)}) %reduce-scatter.3.cloned.1.call-update) | async-done | bytes 196624 | tf_op jit(solution)/shard_map/reduce_scatter | solution.py:112
  301.2 53.1 %all-gather.5.cloned.1.call-done = bf16[1024,1536]{1,0:T(8,128)(2,1)} async-done(((bf16[64,1536]{1,0:T(8,128)(2,1)}), bf16[1024,1536]{1,0:T(8,128)(2,1)}) %all-gather.5.cloned.1.call-update) | async-done | bytes 3145744 | tf_op jit(solution)/shard_map/all_gather | solution.py:122
  354.3 7.2 %convolution_convert_fusion = bf16[1024,1536]{1,0:T(8,128)(2,1)} fusion(bf16[384,1536]{1,0:T(8,128)(2,1)S(1)} %copy-done, bf16[1024,1536]{1,0:T(8,128)(2,1)} %all-gather.5.cloned.1.call-done, bf16[1536,384]{1,0:T(8,128)(2,1)S(1)} %copy-done.11), kind=kOutput, calls=%fused_computation.4 | convolution fusion | flops 2421030912 | bytes 8650752 | tf_op jit(solution)/shard_map/dot_general | solution.py:128
  362.3 79.1 %reduce-scatter.5.cloned.1.call-done = bf16[64,1536]{1,0:T(8,128)(2,1)} async-done(((bf16[1024,1536]{1,0:T(8,128)(2,1)}), bf16[64,1536]{1,0:T(8,128)(2,1)}) %reduce-scatter.5.cloned.1.call-update) | async-done | bytes 196624 | tf_op jit(solution)/shard_map/reduce_scatter | solution.py:127
  (110 shorter events, 52.5 us)
Async XLA Ops:
  7.2 347.1 %copy-start = (bf16[384,1536]{1,0:T(8,128)(2,1)S(1)}, bf16[384,1536]{1,0:T(8,128)(2,1)}, u32[]{:S(2)}) copy-start(bf16[384,1536]{1,0:T(8,128)(2,1)} %param.20) | copy-start | bytes 3538948
  7.2 172.3 %all-gather.3.cloned.1.call-start = ((), (), s32[]{:S(2)}) async-start(), calls=%async_computation.4 | async-start | bytes 6684672 | tf_op jit(solution)/shard_map/all_gather | solution.py:88
  14.2 10.1 %collective-permute-start = (bf16[64,1536]{1,0:T(8,128)(2,1)S(1)}, bf16[64,1536]{1,0:T(8,128)(2,1)S(1)}, u32[]{:S(2)}, u32[]{:S(2)}) collective-permute-start(bf16[64,1536]{1,0:T(8,128)(2,1)S(1)} %get-tuple-element.17), channel_id=1, source_target_pairs={{0,2},{2,4},{4,6},{6,8},{8,10},{10,12},{12,14},{14,16},{16,18},{18... | collective-permute-start | bytes 589832 | tf_op jit(solution)/shard_map/ppermute | solution.py:20
  15.7 8.5 %collective-permute-start.1 = (bf16[64,1536]{1,0:T(8,128)(2,1)S(1)}, bf16[64,1536]{1,0:T(8,128)(2,1)S(1)}, u32[]{:S(2)}, u32[]{:S(2)}) collective-permute-start(bf16[64,1536]{1,0:T(8,128)(2,1)S(1)} %get-tuple-element.17), channel_id=1, source_target_pairs={{0,30},{2,0},{4,2},{6,4},{8,6},{10,8},{12,10},{14,12},{16,14},{18,... | collective-permute-start | bytes 589832 | tf_op jit(solution)/shard_map/ppermute | solution.py:25
  24.3 9.3 %collective-permute-start.2 = (bf16[64,1536]{1,0:T(8,128)(2,1)S(1)}, bf16[64,1536]{1,0:T(8,128)(2,1)S(1)}, u32[]{:S(2)}, u32[]{:S(2)}) collective-permute-start(bf16[64,1536]{1,0:T(8,128)(2,1)S(1)} %collective-permute-done), channel_id=1, source_target_pairs={{0,2},{2,4},{4,6},{6,8},{8,10},{10,12},{12,14},{14,16},{16,18},{18... | collective-permute-start | bytes 589832 | tf_op jit(solution)/shard_map/ppermute | solution.py:20
  24.3 9.3 %collective-permute-start.3 = (bf16[64,1536]{1,0:T(8,128)(2,1)S(1)}, bf16[64,1536]{1,0:T(8,128)(2,1)S(1)}, u32[]{:S(2)}, u32[]{:S(2)}) collective-permute-start(bf16[64,1536]{1,0:T(8,128)(2,1)S(1)} %collective-permute-done.1), channel_id=1, source_target_pairs={{0,30},{2,0},{4,2},{6,4},{8,6},{10,8},{12,10},{14,12},{16,14},{18,... | collective-permute-start | bytes 589832 | tf_op jit(solution)/shard_map/ppermute | solution.py:25
  33.6 9.0 %collective-permute-start.4 = (bf16[64,1536]{1,0:T(8,128)(2,1)S(1)}, bf16[64,1536]{1,0:T(8,128)(2,1)S(1)}, u32[]{:S(2)}, u32[]{:S(2)}) collective-permute-start(bf16[64,1536]{1,0:T(8,128)(2,1)S(1)} %collective-permute-done.2), channel_id=1, source_target_pairs={{0,2},{2,4},{4,6},{6,8},{8,10},{10,12},{12,14},{14,16},{16,18},{18... | collective-permute-start | bytes 589832 | tf_op jit(solution)/shard_map/ppermute | solution.py:20
  33.6 9.0 %collective-permute-start.5 = (bf16[64,1536]{1,0:T(8,128)(2,1)S(1)}, bf16[64,1536]{1,0:T(8,128)(2,1)S(1)}, u32[]{:S(2)}, u32[]{:S(2)}) collective-permute-start(bf16[64,1536]{1,0:T(8,128)(2,1)S(1)} %collective-permute-done.3), channel_id=1, source_target_pairs={{0,30},{2,0},{4,2},{6,4},{8,6},{10,8},{12,10},{14,12},{16,14},{18,... | collective-permute-start | bytes 589832 | tf_op jit(solution)/shard_map/ppermute | solution.py:25
  42.5 9.0 %collective-permute-start.6 = (bf16[64,1536]{1,0:T(8,128)(2,1)S(1)}, bf16[64,1536]{1,0:T(8,128)(2,1)S(1)}, u32[]{:S(2)}, u32[]{:S(2)}) collective-permute-start(bf16[64,1536]{1,0:T(8,128)(2,1)S(1)} %collective-permute-done.4), channel_id=1, source_target_pairs={{0,2},{2,4},{4,6},{6,8},{8,10},{10,12},{12,14},{14,16},{16,18},{18... | collective-permute-start | bytes 589832 | tf_op jit(solution)/shard_map/ppermute | solution.py:20
  42.5 9.0 %collective-permute-start.7 = (bf16[64,1536]{1,0:T(8,128)(2,1)S(1)}, bf16[64,1536]{1,0:T(8,128)(2,1)S(1)}, u32[]{:S(2)}, u32[]{:S(2)}) collective-permute-start(bf16[64,1536]{1,0:T(8,128)(2,1)S(1)} %collective-permute-done.5), channel_id=1, source_target_pairs={{0,30},{2,0},{4,2},{6,4},{8,6},{10,8},{12,10},{14,12},{16,14},{18,... | collective-permute-start | bytes 589832 | tf_op jit(solution)/shard_map/ppermute | solution.py:25
  51.5 9.0 %collective-permute-start.8 = (bf16[64,1536]{1,0:T(8,128)(2,1)S(1)}, bf16[64,1536]{1,0:T(8,128)(2,1)S(1)}, u32[]{:S(2)}, u32[]{:S(2)}) collective-permute-start(bf16[64,1536]{1,0:T(8,128)(2,1)S(1)} %collective-permute-done.6), channel_id=1, source_target_pairs={{0,2},{2,4},{4,6},{6,8},{8,10},{10,12},{12,14},{14,16},{16,18},{18... | collective-permute-start | bytes 589832 | tf_op jit(solution)/shard_map/ppermute | solution.py:20
  51.5 9.0 %collective-permute-start.9 = (bf16[64,1536]{1,0:T(8,128)(2,1)S(1)}, bf16[64,1536]{1,0:T(8,128)(2,1)S(1)}, u32[]{:S(2)}, u32[]{:S(2)}) collective-permute-start(bf16[64,1536]{1,0:T(8,128)(2,1)S(1)} %collective-permute-done.7), channel_id=1, source_target_pairs={{0,30},{2,0},{4,2},{6,4},{8,6},{10,8},{12,10},{14,12},{16,14},{18,... | collective-permute-start | bytes 589832 | tf_op jit(solution)/shard_map/ppermute | solution.py:25
  60.5 9.4 %collective-permute-start.10 = (bf16[64,1536]{1,0:T(8,128)(2,1)S(1)}, bf16[64,1536]{1,0:T(8,128)(2,1)S(1)}, u32[]{:S(2)}, u32[]{:S(2)}) collective-permute-start(bf16[64,1536]{1,0:T(8,128)(2,1)S(1)} %collective-permute-done.8), channel_id=1, source_target_pairs={{0,2},{2,4},{4,6},{6,8},{8,10},{10,12},{12,14},{14,16},{16,18},{18... | collective-permute-start | bytes 589832 | tf_op jit(solution)/shard_map/ppermute | solution.py:20
  60.5 9.4 %collective-permute-start.11 = (bf16[64,1536]{1,0:T(8,128)(2,1)S(1)}, bf16[64,1536]{1,0:T(8,128)(2,1)S(1)}, u32[]{:S(2)}, u32[]{:S(2)}) collective-permute-start(bf16[64,1536]{1,0:T(8,128)(2,1)S(1)} %collective-permute-done.9), channel_id=1, source_target_pairs={{0,30},{2,0},{4,2},{6,4},{8,6},{10,8},{12,10},{14,12},{16,14},{18,... | collective-permute-start | bytes 589832 | tf_op jit(solution)/shard_map/ppermute | solution.py:25
  69.9 10.6 %collective-permute-start.12 = (bf16[64,1536]{1,0:T(8,128)(2,1)S(1)}, bf16[64,1536]{1,0:T(8,128)(2,1)S(1)}, u32[]{:S(2)}, u32[]{:S(2)}) collective-permute-start(bf16[64,1536]{1,0:T(8,128)(2,1)S(1)} %collective-permute-done.10), channel_id=1, source_target_pairs={{0,2},{2,4},{4,6},{6,8},{8,10},{10,12},{12,14},{14,16},{16,18},{18... | collective-permute-start | bytes 589832 | tf_op jit(solution)/shard_map/ppermute | solution.py:20
  69.9 11.3 %collective-permute-start.13 = (bf16[64,1536]{1,0:T(8,128)(2,1)S(1)}, bf16[64,1536]{1,0:T(8,128)(2,1)S(1)}, u32[]{:S(2)}, u32[]{:S(2)}) collective-permute-start(bf16[64,1536]{1,0:T(8,128)(2,1)S(1)} %collective-permute-done.11), channel_id=1, source_target_pairs={{0,30},{2,0},{4,2},{6,4},{8,6},{10,8},{12,10},{14,12},{16,14},{18,... | collective-permute-start | bytes 589832 | tf_op jit(solution)/shard_map/ppermute | solution.py:25
  80.5 9.0 %collective-permute-start.14 = (bf16[64,1536]{1,0:T(8,128)(2,1)S(1)}, bf16[64,1536]{1,0:T(8,128)(2,1)S(1)}, u32[]{:S(2)}, u32[]{:S(2)}) collective-permute-start(bf16[64,1536]{1,0:T(8,128)(2,1)S(1)} %collective-permute-done.12), channel_id=1, source_target_pairs={{0,2},{2,4},{4,6},{6,8},{8,10},{10,12},{12,14},{14,16},{16,18},{18... | collective-permute-start | bytes 589832 | tf_op jit(solution)/shard_map/ppermute | solution.py:20
  113.9 185.0 %reduce-scatter.3.cloned.1.call-start = ((), (), s32[]{:S(2)}) async-start(), calls=%async_computation.5 | async-start | bytes 3342336 | tf_op jit(solution)/shard_map/reduce_scatter | solution.py:112
  216.2 84.1 %copy-start.6 = (f32[1536]{0:T(1024)S(1)}, f32[1536]{0:T(1024)}, u32[]{:S(2)}) copy-start(f32[1536]{0:T(1024)} %get-tuple-element.3) | copy-start | bytes 18436
  216.2 84.1 %copy-start.7 = (f32[1536]{0:T(1024)S(1)}, f32[1536]{0:T(1024)}, u32[]{:S(2)}) copy-start(f32[1536]{0:T(1024)} %get-tuple-element.4) | copy-start | bytes 18436
  219.8 134.4 %copy-start.11 = (bf16[1536,384]{1,0:T(8,128)(2,1)S(1)}, bf16[1536,384]{1,0:T(8,128)(2,1)}, u32[]{:S(2)}) copy-start(bf16[1536,384]{1,0:T(8,128)(2,1)} %param.19) | copy-start | bytes 3538948
  219.8 134.4 %all-gather.5.cloned.1.call-start = ((), (), s32[]{:S(2)}) async-start(), calls=%async_computation.6 | async-start | bytes 3342336 | tf_op jit(solution)/shard_map/all_gather | solution.py:122
  301.2 140.2 %reduce-scatter.5.cloned.1.call-start = ((), (), s32[]{:S(2)}) async-start(), calls=%async_computation.7 | async-start | bytes 3342336 | tf_op jit(solution)/shard_map/reduce_scatter | solution.py:127
  361.5 81.7 %copy-start.8 = (f32[1,32,128]{2,1,0:T(8,128)S(1)}, f32[1,32,128]{2,1,0:T(8,128)}, u32[]{:S(2)}) copy-start(f32[1,32,128]{2,1,0:T(8,128)} %param.12) | copy-start | bytes 49156
  (9 other events, 267.4 us)
Sparse Core Ops, SparseCore 0:
  114.1 65.3 all-gather.2
  220.0 78.9 reduce-scatter.2
  302.0 52.2 all-gather.4
  361.6 79.7 reduce-scatter.4
